TPU v7x, 32 devices: a whole 2x2x4 slice. The times are simulated.
32 devices in a mesh: phase: 16 (over z, y, x), lat: 2 (over core).
Axes of the slice: x: 2, y: 2, z: 4, core: 2. Of those that a mesh axis runs over, the one named last changes fastest.
Arguments:
- state_now: float32 [3, 64, 1024], P(None, ('lat', 'phase')), may hold values from -4 to 4
- ocean_depth: float32 [64, 1024], P('lat'), may hold values from 0.5 to 1.5
- coriolis: float32 [64], P('lat'), may hold values from -0.4 to 0.4
- phase_times: float32 [16], P('phase'), may hold values from -6 to 6
- phase_weights: float32 [16], P('phase'), may hold values from 0.00625 to 0.25
Outputs:
- state_next: float32 [3, 64, 1024], P(None, ('lat', 'phase'))
- tendency: float32 [3, 64, 1024], P(None, ('lat', 'phase'))
All inputs are finite; a program needn't handle non-finite values.
Results may differ from a plain program's by a relative error of at most 0.00002.
Values sent between devices are 32-bit elements; how exact they have to be, the bound alone decides.
A program may use at most 64 MiB of HBM per device.

v0:
```python
import math
import jax
import jax.numpy as jnp
from jax import lax
from jax.sharding import PartitionSpec as P

DEG = 8
DEPTH = 4
radius_scale = 2.5
time_step = 0.5
series_terms = 20


def extended(shard, sides, width):
    for axis, dim in sides:
        devices, length = (lax.axis_size(axis), shard.shape[dim])
        up = [(i, (i + 1) % devices) for i in range(devices - 1)]
        down = [(j, i) for i, j in up]
        last = lax.slice_in_dim(shard, length - width, length, axis=dim)
        first = lax.slice_in_dim(shard, 0, width, axis=dim)
        before = lax.ppermute(last, axis, up)
        after = lax.ppermute(first, axis, down)
        shard = jnp.concatenate([before, shard, after], axis=dim)
    return shard


def along_lon(values):
    return (jnp.roll(values, -1, axis=-1) - jnp.roll(values, 1, axis=-1)) * 0.5


def along_lat(values):
    return (values[..., 2:, :] - values[..., :-2, :]) * 0.5


def interior(values):
    return values[..., 1:-1, :]


def wave_operator(fields, coefficients):
    height = fields[:, 0]
    eastward = fields[:, 1]
    northward = fields[:, 2]
    depth_field = coefficients[0]
    rotation = coefficients[1]
    out_height = -(along_lon(interior(depth_field * eastward)) + along_lat(depth_field * northward))
    out_east = -along_lon(interior(height)) + interior(rotation * northward)
    out_north = -along_lat(height) - interior(rotation * eastward)
    return jnp.stack([out_height, out_east, out_north], axis=1) / radius_scale


def advection(fields):
    height = fields[:, 0]
    eastward = fields[:, 1]
    northward = fields[:, 2]
    mid_east = interior(eastward)
    mid_north = interior(northward)
    out_height = -(along_lon(interior(height * eastward)) + along_lat(height * northward))
    out_east = -(mid_east * along_lon(mid_east) + mid_north * along_lat(eastward))
    out_north = -(mid_east * along_lon(mid_north) + mid_north * along_lat(northward))
    return jnp.stack([out_height, out_east, out_north], axis=1)


def series_coeffs(sample_time):
    half_time = sample_time * 0.5
    square = half_time * half_time
    result = []
    for degree in range(DEG + 1):
        summed = jnp.zeros_like(sample_time)
        term_sq = jnp.ones_like(sample_time)
        for series in range(series_terms):
            factor = (-1.0) ** series / (math.factorial(series) * math.factorial(series + degree))
            summed = summed + factor * term_sq
            term_sq = term_sq * square
        result.append(summed * half_time**degree)
    return result


def trimmed(values, have, wanted):
    excess = have - wanted
    if excess == 0:
        return values
    return values[:, :, excess : values.shape[2] - excess]


def per_device(state_now, ocean_depth, coriolis, phase_times, phase_weights):
    tile_rows = ocean_depth.shape[0]
    lat_count = lax.axis_size("lat")
    lat_place = lax.axis_index("lat")
    stacked = jnp.stack([ocean_depth, jnp.broadcast_to(coriolis[:, None], ocean_depth.shape)])
    coefficients = extended(stacked, (("lat", 1),), DEPTH)
    global_rows = lat_place * tile_rows - DEPTH + jnp.arange(tile_rows + 2 * DEPTH, dtype=jnp.int32)
    inside = ((global_rows >= 0) & (global_rows < tile_rows * lat_count)).astype(jnp.float32)
    forward = series_coeffs(phase_times)
    backward = series_coeffs(-phase_times)
    sample_count = phase_times.shape[0]

    def band_coeffs(margin):
        return coefficients[:, DEPTH - margin : DEPTH + tile_rows + margin]

    def band_inside(margin):
        return inside[DEPTH - margin : DEPTH + tile_rows + margin][None, None, :, None]

    def exponential(fields, series):
        accumulated = series[0][:, None, None, None] * fields
        previous = None
        current = fields
        width_prev = 0
        width_cur = 0
        for degree in range(1, DEG + 1):
            if (degree - 1) % DEPTH == 0:
                if previous is None:
                    current = extended(current, (("lat", 2),), DEPTH)
                else:
                    joined = jnp.concatenate(
                        [trimmed(previous, width_prev, 0), trimmed(current, width_cur, 0)], axis=0
                    )
                    joined = extended(joined, (("lat", 2),), DEPTH)
                    previous = joined[:sample_count]
                    current = joined[sample_count:]
                    width_prev = DEPTH
                width_cur = DEPTH
            width_new = width_cur - 1
            applied = wave_operator(current, band_coeffs(width_cur))
            if previous is None:
                advanced = applied
            else:
                advanced = 2.0 * applied + trimmed(previous, width_prev, width_new)
            advanced = advanced * band_inside(width_new)
            accumulated = accumulated + 2.0 * series[degree][:, None, None, None] * trimmed(
                advanced, width_new, 0
            )
            previous = current
            width_prev = width_cur
            current = advanced
            width_cur = width_new
        return accumulated

    def averaged(whole_tile):
        samples = whole_tile[None]
        waves = exponential(samples, forward)
        rimmed = extended(waves, (("lat", 2),), 1)
        pulled = advection(rimmed)
        returned = exponential(pulled, backward)
        return jnp.sum(phase_weights[:, None, None, None] * returned, axis=0)

    whole_tile = lax.all_gather(state_now, "phase", axis=1, tiled=True)

    def summed_whole(partial_value):
        return lax.psum(partial_value, "phase")

    first = summed_whole(averaged(whole_tile))
    middle = whole_tile + time_step * first
    second = summed_whole(averaged(middle))
    tendency_tile = 0.5 * (first + second)
    share = state_now.shape[1]
    start = lax.axis_index("phase") * share
    tendency = lax.dynamic_slice_in_dim(tendency_tile, start, share, 1)
    state_next = state_now + time_step * tendency
    return (state_next, tendency)


def solution(mesh):
    placed = (P(None, ("lat", "phase"), None), P("lat", None), P("lat"), P("phase"), P("phase"))
    return jax.shard_map(
        per_device,
        mesh=mesh,
        in_specs=placed,
        out_specs=(P(None, ("lat", "phase"), None), P(None, ("lat", "phase"), None)),
        check_vma=False,
    )
```

profile of v0, /device:TPU:0, one launch (start us, length us, event | category | flops | bytes accessed | tf_op | source)
XLA Modules:
  0.0 368.3 jit_solution(13352655160559666389)
XLA Ops:
  8.0 45.3 %all_gather.3 = f32[3,32,1024]{2,0,1:T(4,128)S(1)} all-gather(f32[3,2,1024]{2,0,1:T(4,128)S(1)} %copy.168), channel_id=1, replica_groups=mesh['phase'=16,'lat'=2] {'phase'}, dimensions={1}, use_global_device_ids=true | all-gather | bytes 417792 | tf_op jit(solution)/shard_map/all_gather | solution.py:146
  53.6 1.4 collective-permute-start.3
  55.0 3.0 collective-permute-start.2
  58.2 1.3 collective-permute-start.1
  59.5 3.0 collective-permute-start
  67.0 1.3 collective-permute-start.5
  68.3 3.0 collective-permute-start.4
  76.5 1.3 collective-permute-start.7
  77.8 3.0 collective-permute-start.6
  82.7 1.3 collective-permute-start.9
  84.0 3.0 collective-permute-start.8
  91.5 1.3 collective-permute-start.11
  92.8 3.2 collective-permute-start.10
  100.2 1.3 fusion.41
  101.6 104.9 %all-reduce.3.cloned.1.call-done = f32[3,32,1024]{2,1,0:T(8,128)} async-done(((f32[3,32,1024]{2,1,0:T(8,128)}), f32[3,32,1024]{2,1,0:T(8,128)}) %all-reduce.3.cloned.1.call-update) | async-done | bytes 393232 | tf_op jit(solution)/shard_map/psum | solution.py:149
  207.8 1.3 collective-permute-start.13
  209.1 3.0 collective-permute-start.12
  217.9 3.0 collective-permute-start.14
  228.3 3.0 collective-permute-start.16
  233.2 1.3 collective-permute-start.19
  234.5 3.3 collective-permute-start.18
  243.2 3.0 collective-permute-start.20
  252.0 107.9 %all-reduce.5.cloned.1.call-done = f32[3,32,1024]{2,1,0:T(8,128)} async-done(((f32[3,32,1024]{2,1,0:T(8,128)}), f32[3,32,1024]{2,1,0:T(8,128)}) %all-reduce.5.cloned.1.call-update) | async-done | bytes 393232 | tf_op jit(solution)/shard_map/psum | solution.py:149
  359.9 1.5 multiply_add_fusion.1
  (380 shorter events, 45.4 us)
Async XLA Ops:
  7.2 199.3 %all-reduce.3.cloned.1.call-start = ((), (), s32[]{:S(2)}) async-start(), calls=%async_computation | async-start | bytes 786432 | tf_op jit(solution)/shard_map/psum | solution.py:149
  53.6 9.8 %collective-permute-start.3 = (f32[1,3,4,1024]{3,2,1,0:T(4,128)S(1)}, f32[1,3,4,1024]{3,2,1,0:T(4,128)S(1)}, u32[]{:S(2)}, u32[]{:S(2)}) collective-permute-start(f32[1,3,4,1024]{3,2,1,0:T(4,128)S(1)} %get-tuple-element.195), channel_id=1, source_target_pairs={{1,0},{3,2},{5,4},{7,6},{9,8},{11,10},{13,12},{15,14},{17,16},{19,... | collective-permute-start | bytes 147464 | tf_op jit(solution)/shard_map/ppermute | solution.py:22
  55.0 8.4 %collective-permute-start.2 = (f32[1,3,4,1024]{3,2,1,0:T(4,128)S(1)}, f32[1,3,4,1024]{3,2,1,0:T(4,128)S(1)}, u32[]{:S(2)}, u32[]{:S(2)}) collective-permute-start(f32[1,3,4,1024]{3,2,1,0:T(4,128)S(1)} %get-tuple-element.194), channel_id=1, source_target_pairs={{0,1},{2,3},{4,5},{6,7},{8,9},{10,11},{12,13},{14,15},{16,17},{18,... | collective-permute-start | bytes 147464 | tf_op jit(solution)/shard_map/ppermute | solution.py:21
  58.2 4.6 %collective-permute-start.1 = (f32[2,4,1024]{2,1,0:T(4,128)S(1)}, f32[2,4,1024]{2,1,0:T(4,128)S(1)}, u32[]{:S(2)}, u32[]{:S(2)}) collective-permute-start(f32[2,4,1024]{2,1,0:T(4,128)S(1)} %get-tuple-element.205), channel_id=1, source_target_pairs={{1,0},{3,2},{5,4},{7,6},{9,8},{11,10},{13,12},{15,14},{17,16},{19,... | collective-permute-start | bytes 98312 | tf_op jit(solution)/shard_map/ppermute | solution.py:22
  59.5 3.9 %collective-permute-start = (f32[2,4,1024]{2,1,0:T(4,128)S(1)}, f32[2,4,1024]{2,1,0:T(4,128)S(1)}, u32[]{:S(2)}, u32[]{:S(2)}) collective-permute-start(f32[2,4,1024]{2,1,0:T(4,128)S(1)} %get-tuple-element.204), channel_id=1, source_target_pairs={{0,1},{2,3},{4,5},{6,7},{8,9},{10,11},{12,13},{14,15},{16,17},{18,... | collective-permute-start | bytes 98312 | tf_op jit(solution)/shard_map/ppermute | solution.py:21
  67.0 5.3 %collective-permute-start.5 = (f32[2,3,4,1024]{3,2,1,0:T(4,128)S(1)}, f32[2,3,4,1024]{3,2,1,0:T(4,128)S(1)}, u32[]{:S(2)}, u32[]{:S(2)}) collective-permute-start(f32[2,3,4,1024]{3,2,1,0:T(4,128)S(1)} %get-tuple-element.91), channel_id=1, source_target_pairs={{1,0},{3,2},{5,4},{7,6},{9,8},{11,10},{13,12},{15,14},{17,16},{19,... | collective-permute-start | bytes 294920 | tf_op jit(solution)/shard_map/ppermute | solution.py:22
  68.3 4.0 %collective-permute-start.4 = (f32[2,3,4,1024]{3,2,1,0:T(4,128)S(1)}, f32[2,3,4,1024]{3,2,1,0:T(4,128)S(1)}, u32[]{:S(2)}, u32[]{:S(2)}) collective-permute-start(f32[2,3,4,1024]{3,2,1,0:T(4,128)S(1)} %get-tuple-element.90), channel_id=1, source_target_pairs={{0,1},{2,3},{4,5},{6,7},{8,9},{10,11},{12,13},{14,15},{16,17},{18,... | collective-permute-start | bytes 294920 | tf_op jit(solution)/shard_map/ppermute | solution.py:21
  76.5 4.3 %collective-permute-start.7 = (f32[1,3,1,1024]{3,2,1,0:T(1,128)S(1)}, f32[1,3,1,1024]{3,2,1,0:T(1,128)S(1)}, u32[]{:S(2)}, u32[]{:S(2)}) collective-permute-start(f32[1,3,1,1024]{3,2,1,0:T(1,128)S(1)} %get-tuple-element.193), channel_id=1, source_target_pairs={{1,0},{3,2},{5,4},{7,6},{9,8},{11,10},{13,12},{15,14},{17,16},{19,... | collective-permute-start | bytes 36872 | tf_op jit(solution)/shard_map/ppermute | solution.py:22
  77.8 3.9 %collective-permute-start.6 = (f32[1,3,1,1024]{3,2,1,0:T(1,128)S(1)}, f32[1,3,1,1024]{3,2,1,0:T(1,128)S(1)}, u32[]{:S(2)}, u32[]{:S(2)}) collective-permute-start(f32[1,3,1,1024]{3,2,1,0:T(1,128)S(1)} %get-tuple-element.192), channel_id=1, source_target_pairs={{0,1},{2,3},{4,5},{6,7},{8,9},{10,11},{12,13},{14,15},{16,17},{18,... | collective-permute-start | bytes 36872 | tf_op jit(solution)/shard_map/ppermute | solution.py:21
  82.7 4.3 %collective-permute-start.9 = (f32[1,3,4,1024]{3,2,1,0:T(4,128)S(1)}, f32[1,3,4,1024]{3,2,1,0:T(4,128)S(1)}, u32[]{:S(2)}, u32[]{:S(2)}) collective-permute-start(f32[1,3,4,1024]{3,2,1,0:T(4,128)S(1)} %get-tuple-element.191), channel_id=1, source_target_pairs={{1,0},{3,2},{5,4},{7,6},{9,8},{11,10},{13,12},{15,14},{17,16},{19,... | collective-permute-start | bytes 147464 | tf_op jit(solution)/shard_map/ppermute | solution.py:22
  84.0 3.9 %collective-permute-start.8 = (f32[1,3,4,1024]{3,2,1,0:T(4,128)S(1)}, f32[1,3,4,1024]{3,2,1,0:T(4,128)S(1)}, u32[]{:S(2)}, u32[]{:S(2)}) collective-permute-start(f32[1,3,4,1024]{3,2,1,0:T(4,128)S(1)} %get-tuple-element.190), channel_id=1, source_target_pairs={{0,1},{2,3},{4,5},{6,7},{8,9},{10,11},{12,13},{14,15},{16,17},{18,... | collective-permute-start | bytes 147464 | tf_op jit(solution)/shard_map/ppermute | solution.py:21
  91.5 5.2 %collective-permute-start.11 = (f32[2,3,4,1024]{3,2,1,0:T(4,128)S(1)}, f32[2,3,4,1024]{3,2,1,0:T(4,128)S(1)}, u32[]{:S(2)}, u32[]{:S(2)}) collective-permute-start(f32[2,3,4,1024]{3,2,1,0:T(4,128)S(1)} %get-tuple-element.89), channel_id=1, source_target_pairs={{1,0},{3,2},{5,4},{7,6},{9,8},{11,10},{13,12},{15,14},{17,16},{19,... | collective-permute-start | bytes 294920 | tf_op jit(solution)/shard_map/ppermute | solution.py:22
  92.8 4.0 %collective-permute-start.10 = (f32[2,3,4,1024]{3,2,1,0:T(4,128)S(1)}, f32[2,3,4,1024]{3,2,1,0:T(4,128)S(1)}, u32[]{:S(2)}, u32[]{:S(2)}) collective-permute-start(f32[2,3,4,1024]{3,2,1,0:T(4,128)S(1)} %get-tuple-element.88), channel_id=1, source_target_pairs={{0,1},{2,3},{4,5},{6,7},{8,9},{10,11},{12,13},{14,15},{16,17},{18,... | collective-permute-start | bytes 294920 | tf_op jit(solution)/shard_map/ppermute | solution.py:21
  101.6 258.3 %all-reduce.5.cloned.1.call-start = ((), (), s32[]{:S(2)}) async-start(), calls=%async_computation.1 | async-start | bytes 786432 | tf_op jit(solution)/shard_map/psum | solution.py:149
  207.8 4.3 %collective-permute-start.13 = (f32[1,3,4,1024]{3,2,1,0:T(4,128)S(1)}, f32[1,3,4,1024]{3,2,1,0:T(4,128)S(1)}, u32[]{:S(2)}, u32[]{:S(2)}) collective-permute-start(f32[1,3,4,1024]{3,2,1,0:T(4,128)S(1)} %get-tuple-element.189), channel_id=1, source_target_pairs={{1,0},{3,2},{5,4},{7,6},{9,8},{11,10},{13,12},{15,14},{17,16},{19,... | collective-permute-start | bytes 147464 | tf_op jit(solution)/shard_map/ppermute | solution.py:22
  209.1 3.9 %collective-permute-start.12 = (f32[1,3,4,1024]{3,2,1,0:T(4,128)S(1)}, f32[1,3,4,1024]{3,2,1,0:T(4,128)S(1)}, u32[]{:S(2)}, u32[]{:S(2)}) collective-permute-start(f32[1,3,4,1024]{3,2,1,0:T(4,128)S(1)} %get-tuple-element.188), channel_id=1, source_target_pairs={{0,1},{2,3},{4,5},{6,7},{8,9},{10,11},{12,13},{14,15},{16,17},{18,... | collective-permute-start | bytes 147464 | tf_op jit(solution)/shard_map/ppermute | solution.py:21
  216.6 4.3 %collective-permute-start.15 = (f32[2,3,4,1024]{3,2,1,0:T(4,128)S(1)}, f32[2,3,4,1024]{3,2,1,0:T(4,128)S(1)}, u32[]{:S(2)}, u32[]{:S(2)}) collective-permute-start(f32[2,3,4,1024]{3,2,1,0:T(4,128)S(1)} %get-tuple-element.87), channel_id=1, source_target_pairs={{1,0},{3,2},{5,4},{7,6},{9,8},{11,10},{13,12},{15,14},{17,16},{19,... | collective-permute-start | bytes 294920 | tf_op jit(solution)/shard_map/ppermute | solution.py:22
  217.9 4.0 %collective-permute-start.14 = (f32[2,3,4,1024]{3,2,1,0:T(4,128)S(1)}, f32[2,3,4,1024]{3,2,1,0:T(4,128)S(1)}, u32[]{:S(2)}, u32[]{:S(2)}) collective-permute-start(f32[2,3,4,1024]{3,2,1,0:T(4,128)S(1)} %get-tuple-element.86), channel_id=1, source_target_pairs={{0,1},{2,3},{4,5},{6,7},{8,9},{10,11},{12,13},{14,15},{16,17},{18,... | collective-permute-start | bytes 294920 | tf_op jit(solution)/shard_map/ppermute | solution.py:21
  227.0 4.3 %collective-permute-start.17 = (f32[1,3,1,1024]{3,2,1,0:T(1,128)S(1)}, f32[1,3,1,1024]{3,2,1,0:T(1,128)S(1)}, u32[]{:S(2)}, u32[]{:S(2)}) collective-permute-start(f32[1,3,1,1024]{3,2,1,0:T(1,128)S(1)} %get-tuple-element.187), channel_id=1, source_target_pairs={{1,0},{3,2},{5,4},{7,6},{9,8},{11,10},{13,12},{15,14},{17,16},{19,... | collective-permute-start | bytes 36872 | tf_op jit(solution)/shard_map/ppermute | solution.py:22
  228.3 3.9 %collective-permute-start.16 = (f32[1,3,1,1024]{3,2,1,0:T(1,128)S(1)}, f32[1,3,1,1024]{3,2,1,0:T(1,128)S(1)}, u32[]{:S(2)}, u32[]{:S(2)}) collective-permute-start(f32[1,3,1,1024]{3,2,1,0:T(1,128)S(1)} %get-tuple-element.186), channel_id=1, source_target_pairs={{0,1},{2,3},{4,5},{6,7},{8,9},{10,11},{12,13},{14,15},{16,17},{18,... | collective-permute-start | bytes 36872 | tf_op jit(solution)/shard_map/ppermute | solution.py:21
  233.2 4.6 %collective-permute-start.19 = (f32[1,3,4,1024]{3,2,1,0:T(4,128)S(1)}, f32[1,3,4,1024]{3,2,1,0:T(4,128)S(1)}, u32[]{:S(2)}, u32[]{:S(2)}) collective-permute-start(f32[1,3,4,1024]{3,2,1,0:T(4,128)S(1)} %get-tuple-element.185), channel_id=1, source_target_pairs={{1,0},{3,2},{5,4},{7,6},{9,8},{11,10},{13,12},{15,14},{17,16},{19,... | collective-permute-start | bytes 147464 | tf_op jit(solution)/shard_map/ppermute | solution.py:22
  234.5 3.9 %collective-permute-start.18 = (f32[1,3,4,1024]{3,2,1,0:T(4,128)S(1)}, f32[1,3,4,1024]{3,2,1,0:T(4,128)S(1)}, u32[]{:S(2)}, u32[]{:S(2)}) collective-permute-start(f32[1,3,4,1024]{3,2,1,0:T(4,128)S(1)} %get-tuple-element.184), channel_id=1, source_target_pairs={{0,1},{2,3},{4,5},{6,7},{8,9},{10,11},{12,13},{14,15},{16,17},{18,... | collective-permute-start | bytes 147464 | tf_op jit(solution)/shard_map/ppermute | solution.py:21
  241.9 4.3 %collective-permute-start.21 = (f32[2,3,4,1024]{3,2,1,0:T(4,128)S(1)}, f32[2,3,4,1024]{3,2,1,0:T(4,128)S(1)}, u32[]{:S(2)}, u32[]{:S(2)}) collective-permute-start(f32[2,3,4,1024]{3,2,1,0:T(4,128)S(1)} %get-tuple-element.85), channel_id=1, source_target_pairs={{1,0},{3,2},{5,4},{7,6},{9,8},{11,10},{13,12},{15,14},{17,16},{19,... | collective-permute-start | bytes 294920 | tf_op jit(solution)/shard_map/ppermute | solution.py:22
  243.2 4.0 %collective-permute-start.20 = (f32[2,3,4,1024]{3,2,1,0:T(4,128)S(1)}, f32[2,3,4,1024]{3,2,1,0:T(4,128)S(1)}, u32[]{:S(2)}, u32[]{:S(2)}) collective-permute-start(f32[2,3,4,1024]{3,2,1,0:T(4,128)S(1)} %get-tuple-element.84), channel_id=1, source_target_pairs={{0,1},{2,3},{4,5},{6,7},{8,9},{10,11},{12,13},{14,15},{16,17},{18,... | collective-permute-start | bytes 294920 | tf_op jit(solution)/shard_map/ppermute | solution.py:21
  (4 other events, 118.0 us)
Sparse Core Ops, SparseCore 0:
  101.7 104.7 all-reduce.2
  252.1 107.7 all-reduce.4
where the time goes:
time: 369 us; the launch traced here: 368 us
  waiting for transfers between devices  219 us (59%)
  starting transfers between devices  48.2 us (13%)
  blocking collectives  45.3 us (12%)
  other arithmetic  21.8 us (6%)
  between operations  17.7 us (5%)
  local copies, waits for them, and re-layouts  16.1 us (4%)
    psum x2, waiting for transfers between devices, summed_whole(): return lax.psum(partial_value, 'phase')  213 us
    all_gather x1, blocking collectives, per_device(): whole_tile = lax.all_gather(state_now, 'phase', axis=1, tiled=True)  45.3 us
    ppermute x11, starting transfers between devices, extended(): before = lax.ppermute(last, axis, up)  33.8 us
    ppermute x11, starting transfers between devices, extended(): after = lax.ppermute(first, axis, down)  14.3 us
    slice x140, local copies, waits for them, and re-layouts, along_lon(): return (jnp.roll(values, -1, axis=-1) - jnp.roll(values, 1, axis=-1)) * 0.5  12.7 us
    another operation x63, other arithmetic, wave_operator(): return jnp.stack([out_height, out_east, out_north], axis=1) / radius_scale  7.91 us
  transfers between devices with their start and end apart: 24, of which 10 were waited for; matrix products, arithmetic and copies ran while one was open for 0% of the time, Pallas kernels for 0%

commit v1 on v0

--- a/solution.py
+++ b/solution.py
@@ -143,7 +143,7 @@
         returned = exponential(pulled, backward)
         return jnp.sum(phase_weights[:, None, None, None] * returned, axis=0)
 
-    whole_tile = lax.all_gather(state_now, "phase", axis=1, tiled=True)
+    whole_tile = jnp.concatenate(lax.all_gather(state_now, "phase"), axis=1)
 
     def summed_whole(partial_value):
         return lax.psum(partial_value, "phase")

time: 369 us -> 367 us (level)
  no operation moved by 1% of the time
where the time goes in v1:
time: 367 us; the launch traced here: 366 us
  waiting for transfers between devices  219 us (60%)
  starting transfers between devices  48.2 us (13%)
  blocking collectives  44.7 us (12%)
  other arithmetic  21.2 us (6%)
  between operations  17.7 us (5%)
  local copies, waits for them, and re-layouts  15.7 us (4%)
    psum x2, waiting for transfers between devices, summed_whole(): return lax.psum(partial_value, 'phase')  212 us
    all_gather x1, blocking collectives, per_device(): whole_tile = jnp.concatenate(lax.all_gather(state_now, 'phase'), axis=1)  44.7 us
    ppermute x11, starting transfers between devices, extended(): before = lax.ppermute(last, axis, up)  33.8 us
    ppermute x11, starting transfers between devices, extended(): after = lax.ppermute(first, axis, down)  14.3 us
    slice x140, local copies, waits for them, and re-layouts, along_lon(): return (jnp.roll(values, -1, axis=-1) - jnp.roll(values, 1, axis=-1)) * 0.5  12.7 us
    another operation x63, other arithmetic, wave_operator(): return jnp.stack([out_height, out_east, out_north], axis=1) / radius_scale  7.92 us
  transfers between devices with their start and end apart: 24, of which 10 were waited for; matrix products, arithmetic and copies ran while one was open for 0% of the time, Pallas kernels for 0%

profile of v1, /device:TPU:0, one launch (start us, length us, event | category | flops | bytes accessed | tf_op | source)
XLA Modules:
  0.0 366.4 jit_solution(15152447900863589484)
XLA Ops:
  7.2 44.7 %all-gather = f32[48,2,1024]{2,1,0:T(2,128)S(1)} all-gather(f32[3,2,1024]{2,1,0:T(2,128)} %param.5), channel_id=2, replica_groups=mesh['phase'=16,'lat'=2] {'phase'}, dimensions={0}, use_global_device_ids=true | all-gather | bytes 417792 | tf_op jit(solution)/shard_map/all_gather | solution.py:146
  52.3 1.4 collective-permute-start.3
  53.8 3.0 collective-permute-start.2
  56.9 1.3 collective-permute-start.1
  58.2 3.0 collective-permute-start
  65.7 1.3 collective-permute-start.5
  67.0 3.0 collective-permute-start.4
  75.1 1.3 collective-permute-start.7
  76.4 3.0 collective-permute-start.6
  81.3 1.3 collective-permute-start.9
  82.6 3.0 collective-permute-start.8
  90.0 1.3 collective-permute-start.11
  91.3 3.2 collective-permute-start.10
  98.8 1.3 fusion.41
  100.4 104.6 %all-reduce.3.cloned.1.call-done = f32[3,32,1024]{2,1,0:T(8,128)} async-done(((f32[3,32,1024]{2,1,0:T(8,128)}), f32[3,32,1024]{2,1,0:T(8,128)}) %all-reduce.3.cloned.1.call-update) | async-done | bytes 393232 | tf_op jit(solution)/shard_map/psum | solution.py:149
  206.1 1.3 collective-permute-start.13
  207.4 3.0 collective-permute-start.12
  216.2 3.0 collective-permute-start.14
  226.5 3.0 collective-permute-start.16
  232.6 3.3 collective-permute-start.18
  240.1 1.3 collective-permute-start.21
  241.4 3.0 collective-permute-start.20
  250.2 107.9 %all-reduce.5.cloned.1.call-done = f32[3,32,1024]{2,1,0:T(8,128)} async-done(((f32[3,32,1024]{2,1,0:T(8,128)}), f32[3,32,1024]{2,1,0:T(8,128)}) %all-reduce.5.cloned.1.call-update) | async-done | bytes 393232 | tf_op jit(solution)/shard_map/psum | solution.py:149
  358.1 1.5 multiply_add_fusion.1
  (381 shorter events, 44.4 us)
Async XLA Ops:
  7.2 197.9 %all-reduce.3.cloned.1.call-start = ((), (), s32[]{:S(2)}) async-start(), calls=%async_computation | async-start | bytes 786432 | tf_op jit(solution)/shard_map/psum | solution.py:149
  52.3 9.8 %collective-permute-start.3 = (f32[1,3,4,1024]{3,2,1,0:T(4,128)S(1)}, f32[1,3,4,1024]{3,2,1,0:T(4,128)S(1)}, u32[]{:S(2)}, u32[]{:S(2)}) collective-permute-start(f32[1,3,4,1024]{3,2,1,0:T(4,128)S(1)} %get-tuple-element.195), channel_id=1, source_target_pairs={{1,0},{3,2},{5,4},{7,6},{9,8},{11,10},{13,12},{15,14},{17,16},{19,... | collective-permute-start | bytes 147464 | tf_op jit(solution)/shard_map/ppermute | solution.py:22
  53.8 8.4 %collective-permute-start.2 = (f32[1,3,4,1024]{3,2,1,0:T(4,128)S(1)}, f32[1,3,4,1024]{3,2,1,0:T(4,128)S(1)}, u32[]{:S(2)}, u32[]{:S(2)}) collective-permute-start(f32[1,3,4,1024]{3,2,1,0:T(4,128)S(1)} %get-tuple-element.194), channel_id=1, source_target_pairs={{0,1},{2,3},{4,5},{6,7},{8,9},{10,11},{12,13},{14,15},{16,17},{18,... | collective-permute-start | bytes 147464 | tf_op jit(solution)/shard_map/ppermute | solution.py:21
  56.9 4.6 %collective-permute-start.1 = (f32[2,4,1024]{2,1,0:T(4,128)S(1)}, f32[2,4,1024]{2,1,0:T(4,128)S(1)}, u32[]{:S(2)}, u32[]{:S(2)}) collective-permute-start(f32[2,4,1024]{2,1,0:T(4,128)S(1)} %get-tuple-element.205), channel_id=1, source_target_pairs={{1,0},{3,2},{5,4},{7,6},{9,8},{11,10},{13,12},{15,14},{17,16},{19,... | collective-permute-start | bytes 98312 | tf_op jit(solution)/shard_map/ppermute | solution.py:22
  58.2 3.9 %collective-permute-start = (f32[2,4,1024]{2,1,0:T(4,128)S(1)}, f32[2,4,1024]{2,1,0:T(4,128)S(1)}, u32[]{:S(2)}, u32[]{:S(2)}) collective-permute-start(f32[2,4,1024]{2,1,0:T(4,128)S(1)} %get-tuple-element.204), channel_id=1, source_target_pairs={{0,1},{2,3},{4,5},{6,7},{8,9},{10,11},{12,13},{14,15},{16,17},{18,... | collective-permute-start | bytes 98312 | tf_op jit(solution)/shard_map/ppermute | solution.py:21
  65.7 5.3 %collective-permute-start.5 = (f32[2,3,4,1024]{3,2,1,0:T(4,128)S(1)}, f32[2,3,4,1024]{3,2,1,0:T(4,128)S(1)}, u32[]{:S(2)}, u32[]{:S(2)}) collective-permute-start(f32[2,3,4,1024]{3,2,1,0:T(4,128)S(1)} %get-tuple-element.91), channel_id=1, source_target_pairs={{1,0},{3,2},{5,4},{7,6},{9,8},{11,10},{13,12},{15,14},{17,16},{19,... | collective-permute-start | bytes 294920 | tf_op jit(solution)/shard_map/ppermute | solution.py:22
  67.0 4.0 %collective-permute-start.4 = (f32[2,3,4,1024]{3,2,1,0:T(4,128)S(1)}, f32[2,3,4,1024]{3,2,1,0:T(4,128)S(1)}, u32[]{:S(2)}, u32[]{:S(2)}) collective-permute-start(f32[2,3,4,1024]{3,2,1,0:T(4,128)S(1)} %get-tuple-element.90), channel_id=1, source_target_pairs={{0,1},{2,3},{4,5},{6,7},{8,9},{10,11},{12,13},{14,15},{16,17},{18,... | collective-permute-start | bytes 294920 | tf_op jit(solution)/shard_map/ppermute | solution.py:21
  75.1 4.3 %collective-permute-start.7 = (f32[1,3,1,1024]{3,2,1,0:T(1,128)S(1)}, f32[1,3,1,1024]{3,2,1,0:T(1,128)S(1)}, u32[]{:S(2)}, u32[]{:S(2)}) collective-permute-start(f32[1,3,1,1024]{3,2,1,0:T(1,128)S(1)} %get-tuple-element.193), channel_id=1, source_target_pairs={{1,0},{3,2},{5,4},{7,6},{9,8},{11,10},{13,12},{15,14},{17,16},{19,... | collective-permute-start | bytes 36872 | tf_op jit(solution)/shard_map/ppermute | solution.py:22
  76.4 3.9 %collective-permute-start.6 = (f32[1,3,1,1024]{3,2,1,0:T(1,128)S(1)}, f32[1,3,1,1024]{3,2,1,0:T(1,128)S(1)}, u32[]{:S(2)}, u32[]{:S(2)}) collective-permute-start(f32[1,3,1,1024]{3,2,1,0:T(1,128)S(1)} %get-tuple-element.192), channel_id=1, source_target_pairs={{0,1},{2,3},{4,5},{6,7},{8,9},{10,11},{12,13},{14,15},{16,17},{18,... | collective-permute-start | bytes 36872 | tf_op jit(solution)/shard_map/ppermute | solution.py:21
  81.3 4.3 %collective-permute-start.9 = (f32[1,3,4,1024]{3,2,1,0:T(4,128)S(1)}, f32[1,3,4,1024]{3,2,1,0:T(4,128)S(1)}, u32[]{:S(2)}, u32[]{:S(2)}) collective-permute-start(f32[1,3,4,1024]{3,2,1,0:T(4,128)S(1)} %get-tuple-element.191), channel_id=1, source_target_pairs={{1,0},{3,2},{5,4},{7,6},{9,8},{11,10},{13,12},{15,14},{17,16},{19,... | collective-permute-start | bytes 147464 | tf_op jit(solution)/shard_map/ppermute | solution.py:22
  82.6 3.9 %collective-permute-start.8 = (f32[1,3,4,1024]{3,2,1,0:T(4,128)S(1)}, f32[1,3,4,1024]{3,2,1,0:T(4,128)S(1)}, u32[]{:S(2)}, u32[]{:S(2)}) collective-permute-start(f32[1,3,4,1024]{3,2,1,0:T(4,128)S(1)} %get-tuple-element.190), channel_id=1, source_target_pairs={{0,1},{2,3},{4,5},{6,7},{8,9},{10,11},{12,13},{14,15},{16,17},{18,... | collective-permute-start | bytes 147464 | tf_op jit(solution)/shard_map/ppermute | solution.py:21
  90.0 5.2 %collective-permute-start.11 = (f32[2,3,4,1024]{3,2,1,0:T(4,128)S(1)}, f32[2,3,4,1024]{3,2,1,0:T(4,128)S(1)}, u32[]{:S(2)}, u32[]{:S(2)}) collective-permute-start(f32[2,3,4,1024]{3,2,1,0:T(4,128)S(1)} %get-tuple-element.89), channel_id=1, source_target_pairs={{1,0},{3,2},{5,4},{7,6},{9,8},{11,10},{13,12},{15,14},{17,16},{19,... | collective-permute-start | bytes 294920 | tf_op jit(solution)/shard_map/ppermute | solution.py:22
  91.3 4.0 %collective-permute-start.10 = (f32[2,3,4,1024]{3,2,1,0:T(4,128)S(1)}, f32[2,3,4,1024]{3,2,1,0:T(4,128)S(1)}, u32[]{:S(2)}, u32[]{:S(2)}) collective-permute-start(f32[2,3,4,1024]{3,2,1,0:T(4,128)S(1)} %get-tuple-element.88), channel_id=1, source_target_pairs={{0,1},{2,3},{4,5},{6,7},{8,9},{10,11},{12,13},{14,15},{16,17},{18,... | collective-permute-start | bytes 294920 | tf_op jit(solution)/shard_map/ppermute | solution.py:21
  100.1 257.9 %all-reduce.5.cloned.1.call-start = ((), (), s32[]{:S(2)}) async-start(), calls=%async_computation.1 | async-start | bytes 786432 | tf_op jit(solution)/shard_map/psum | solution.py:149
  206.1 4.3 %collective-permute-start.13 = (f32[1,3,4,1024]{3,2,1,0:T(4,128)S(1)}, f32[1,3,4,1024]{3,2,1,0:T(4,128)S(1)}, u32[]{:S(2)}, u32[]{:S(2)}) collective-permute-start(f32[1,3,4,1024]{3,2,1,0:T(4,128)S(1)} %get-tuple-element.189), channel_id=1, source_target_pairs={{1,0},{3,2},{5,4},{7,6},{9,8},{11,10},{13,12},{15,14},{17,16},{19,... | collective-permute-start | bytes 147464 | tf_op jit(solution)/shard_map/ppermute | solution.py:22
  207.4 3.9 %collective-permute-start.12 = (f32[1,3,4,1024]{3,2,1,0:T(4,128)S(1)}, f32[1,3,4,1024]{3,2,1,0:T(4,128)S(1)}, u32[]{:S(2)}, u32[]{:S(2)}) collective-permute-start(f32[1,3,4,1024]{3,2,1,0:T(4,128)S(1)} %get-tuple-element.188), channel_id=1, source_target_pairs={{0,1},{2,3},{4,5},{6,7},{8,9},{10,11},{12,13},{14,15},{16,17},{18,... | collective-permute-start | bytes 147464 | tf_op jit(solution)/shard_map/ppermute | solution.py:21
  214.9 4.3 %collective-permute-start.15 = (f32[2,3,4,1024]{3,2,1,0:T(4,128)S(1)}, f32[2,3,4,1024]{3,2,1,0:T(4,128)S(1)}, u32[]{:S(2)}, u32[]{:S(2)}) collective-permute-start(f32[2,3,4,1024]{3,2,1,0:T(4,128)S(1)} %get-tuple-element.87), channel_id=1, source_target_pairs={{1,0},{3,2},{5,4},{7,6},{9,8},{11,10},{13,12},{15,14},{17,16},{19,... | collective-permute-start | bytes 294920 | tf_op jit(solution)/shard_map/ppermute | solution.py:22
  216.2 4.0 %collective-permute-start.14 = (f32[2,3,4,1024]{3,2,1,0:T(4,128)S(1)}, f32[2,3,4,1024]{3,2,1,0:T(4,128)S(1)}, u32[]{:S(2)}, u32[]{:S(2)}) collective-permute-start(f32[2,3,4,1024]{3,2,1,0:T(4,128)S(1)} %get-tuple-element.86), channel_id=1, source_target_pairs={{0,1},{2,3},{4,5},{6,7},{8,9},{10,11},{12,13},{14,15},{16,17},{18,... | collective-permute-start | bytes 294920 | tf_op jit(solution)/shard_map/ppermute | solution.py:21
  225.2 4.3 %collective-permute-start.17 = (f32[1,3,1,1024]{3,2,1,0:T(1,128)S(1)}, f32[1,3,1,1024]{3,2,1,0:T(1,128)S(1)}, u32[]{:S(2)}, u32[]{:S(2)}) collective-permute-start(f32[1,3,1,1024]{3,2,1,0:T(1,128)S(1)} %get-tuple-element.187), channel_id=1, source_target_pairs={{1,0},{3,2},{5,4},{7,6},{9,8},{11,10},{13,12},{15,14},{17,16},{19,... | collective-permute-start | bytes 36872 | tf_op jit(solution)/shard_map/ppermute | solution.py:22
  226.5 3.9 %collective-permute-start.16 = (f32[1,3,1,1024]{3,2,1,0:T(1,128)S(1)}, f32[1,3,1,1024]{3,2,1,0:T(1,128)S(1)}, u32[]{:S(2)}, u32[]{:S(2)}) collective-permute-start(f32[1,3,1,1024]{3,2,1,0:T(1,128)S(1)} %get-tuple-element.186), channel_id=1, source_target_pairs={{0,1},{2,3},{4,5},{6,7},{8,9},{10,11},{12,13},{14,15},{16,17},{18,... | collective-permute-start | bytes 36872 | tf_op jit(solution)/shard_map/ppermute | solution.py:21
  231.3 4.6 %collective-permute-start.19 = (f32[1,3,4,1024]{3,2,1,0:T(4,128)S(1)}, f32[1,3,4,1024]{3,2,1,0:T(4,128)S(1)}, u32[]{:S(2)}, u32[]{:S(2)}) collective-permute-start(f32[1,3,4,1024]{3,2,1,0:T(4,128)S(1)} %get-tuple-element.185), channel_id=1, source_target_pairs={{1,0},{3,2},{5,4},{7,6},{9,8},{11,10},{13,12},{15,14},{17,16},{19,... | collective-permute-start | bytes 147464 | tf_op jit(solution)/shard_map/ppermute | solution.py:22
  232.6 3.9 %collective-permute-start.18 = (f32[1,3,4,1024]{3,2,1,0:T(4,128)S(1)}, f32[1,3,4,1024]{3,2,1,0:T(4,128)S(1)}, u32[]{:S(2)}, u32[]{:S(2)}) collective-permute-start(f32[1,3,4,1024]{3,2,1,0:T(4,128)S(1)} %get-tuple-element.184), channel_id=1, source_target_pairs={{0,1},{2,3},{4,5},{6,7},{8,9},{10,11},{12,13},{14,15},{16,17},{18,... | collective-permute-start | bytes 147464 | tf_op jit(solution)/shard_map/ppermute | solution.py:21
  240.1 4.3 %collective-permute-start.21 = (f32[2,3,4,1024]{3,2,1,0:T(4,128)S(1)}, f32[2,3,4,1024]{3,2,1,0:T(4,128)S(1)}, u32[]{:S(2)}, u32[]{:S(2)}) collective-permute-start(f32[2,3,4,1024]{3,2,1,0:T(4,128)S(1)} %get-tuple-element.85), channel_id=1, source_target_pairs={{1,0},{3,2},{5,4},{7,6},{9,8},{11,10},{13,12},{15,14},{17,16},{19,... | collective-permute-start | bytes 294920 | tf_op jit(solution)/shard_map/ppermute | solution.py:22
  241.4 4.0 %collective-permute-start.20 = (f32[2,3,4,1024]{3,2,1,0:T(4,128)S(1)}, f32[2,3,4,1024]{3,2,1,0:T(4,128)S(1)}, u32[]{:S(2)}, u32[]{:S(2)}) collective-permute-start(f32[2,3,4,1024]{3,2,1,0:T(4,128)S(1)} %get-tuple-element.84), channel_id=1, source_target_pairs={{0,1},{2,3},{4,5},{6,7},{8,9},{10,11},{12,13},{14,15},{16,17},{18,... | collective-permute-start | bytes 294920 | tf_op jit(solution)/shard_map/ppermute | solution.py:21
  (4 other events, 118.0 us)
Sparse Core Ops, SparseCore 0:
  100.2 104.7 all-reduce.2
  250.3 107.7 all-reduce.4
